TPU v7x, 256 devices: a whole 4x4x8 slice. The times are simulated.
256 devices in a mesh: ctx: 16 (over z, x_lo), seq: 16 (over y, x_hi, core).
Axes of the slice: x: 4 (x_hi: 2, x_lo: 2; x = x_hi * 2 + x_lo), y: 4, z: 8, core: 2. Of those that a mesh axis runs over, the one named last changes fastest.
Arguments:
- normed_hidden_input: bfloat16 [16, 2048, 4096], P('seq', 'ctx'), may hold values from -6 to 6
- frozen_query_base: bfloat16 [16, 2048, 2048], P('seq', 'ctx'), may hold values from -6 to 6
- key_head_states: bfloat16 [16, 2048, 512], P('seq', 'ctx'), may hold values from -6 to 6
- value_head_states: bfloat16 [16, 2048, 512], P('seq', 'ctx'), may hold values from -6 to 6
- document_numbers: int32 [16, 2048], P('seq', 'ctx'), may hold values from 0 to 3, as said below
- tenant_block_entry: int32 [16, 64], P('seq', 'ctx'), may hold values from 0 to 5
- sequence_adapter_list: int32 [16, 6], replicated, may hold values from 0 to 15, as said below
- adapter_down_weight: bfloat16 [16, 64, 4096], P('seq', None, 'ctx'), may hold values from -0.09375 to 0.09375
- adapter_up_weight: bfloat16 [16, 64, 2048], P('seq', None, 'ctx'), may hold values from -0.75 to 0.75
- output_gradient: bfloat16 [16, 2048, 2048], P('seq', 'ctx'), may hold values from -6 to 6
Outputs:
- attention_out: bfloat16 [16, 2048, 2048], P('seq', 'ctx')
- key_grad: float32 [16, 2048, 512], P('seq', 'ctx')
- value_grad: float32 [16, 2048, 512], P('seq', 'ctx')
- down_grad: float32 [16, 64, 4096], P('seq', None, 'ctx')
- up_grad: float32 [16, 64, 2048], P('seq', None, 'ctx')
Inputs may be any that keep to these rules, and one draw needn't show every extreme that they name: `document_numbers`: each sequence is cut into 4 documents of consecutive positions, numbered in order; every document starts at an even position and has 2 or more positions. `sequence_adapter_list`: each row lists 6 different tenants.
All inputs are finite; a program needn't handle non-finite values.
Results may differ from a plain program's by a relative error of at most 0.04.
Values may be sent and summed in bfloat16 or wider, within the bound.
A program may use at most 128 MiB of HBM per device.

v0:
```python
import math
import jax
import jax.numpy as jnp
from jax import lax
from jax.sharding import PartitionSpec as P

MODEL_WIDTH = 4096
QUERY_HEADS = 16
KEY_VALUE_HEADS = 4
HEAD_SIZE = 128
ADAPTER_RANK = 64
TB = 32
PICK = 6
masked_fill_value = -1e30


def forward_block(
    running,
    query_head_rows,
    query_pos,
    query_doc,
    key_block,
    value_block,
    doc_block,
    key_pos,
    score_scale,
):
    row_peak, weight_total, mixed_sum = running
    scores = (
        jnp.einsum("tkgd,skd->kgts", query_head_rows, key_block, preferred_element_type=jnp.float32)
        * score_scale
    )
    allowed = (query_doc[:, None] == doc_block[None, :]) & (key_pos[None, :] <= query_pos[:, None])
    scores = jnp.where(allowed, scores, masked_fill_value)
    new_peak = jnp.maximum(row_peak, jnp.max(scores, axis=-1))
    weights = jnp.where(allowed, jnp.exp(scores - new_peak[..., None]), 0.0)
    factor = jnp.exp(row_peak - new_peak)
    weight_total = weight_total * factor + jnp.sum(weights, axis=-1)
    mixed_sum = mixed_sum * factor[..., None] + jnp.einsum(
        "kgts,skd->kgtd",
        weights.astype(jnp.bfloat16),
        value_block,
        preferred_element_type=jnp.float32,
    )
    return (new_peak, weight_total, mixed_sum)


def backward_block(
    query_head_rows,
    gradient_head_rows,
    query_pos,
    query_doc,
    log_total,
    delta_sum,
    key_block,
    value_block,
    doc_block,
    key_pos,
    score_scale,
):
    scores = (
        jnp.einsum("tkgd,skd->kgts", query_head_rows, key_block, preferred_element_type=jnp.float32)
        * score_scale
    )
    allowed = (query_doc[:, None] == doc_block[None, :]) & (key_pos[None, :] <= query_pos[:, None])
    probabilities = jnp.where(
        allowed, jnp.exp(jnp.where(allowed, scores, masked_fill_value) - log_total[..., None]), 0.0
    )
    value_part = jnp.einsum(
        "kgts,tkgd->skd",
        probabilities.astype(jnp.bfloat16),
        gradient_head_rows,
        preferred_element_type=jnp.float32,
    )
    dprobs = jnp.einsum(
        "tkgd,skd->kgts", gradient_head_rows, value_block, preferred_element_type=jnp.float32
    )
    dscores = (probabilities * (dprobs - delta_sum[..., None])).astype(jnp.bfloat16)
    query_part = score_scale * jnp.einsum(
        "kgts,skd->kgtd", dscores, key_block, preferred_element_type=jnp.float32
    )
    key_part = score_scale * jnp.einsum(
        "kgts,tkgd->skd", dscores, query_head_rows, preferred_element_type=jnp.float32
    )
    return (query_part, key_part, value_part)


def per_device(
    normed_hidden_input,
    frozen_query_base,
    key_head_states,
    value_head_states,
    document_numbers,
    tenant_block_entry,
    sequence_adapter_list,
    adapter_down_weight,
    adapter_up_weight,
    output_gradient,
):
    cycle_count = lax.axis_size("ctx")
    cycle_index = lax.axis_index("ctx")
    group_index = lax.axis_index("seq")
    tokens = normed_hidden_input[0]
    row_total_count = tokens.shape[0]
    seq_len = row_total_count * cycle_count
    head_groupings = QUERY_HEADS // KEY_VALUE_HEADS
    query_width = QUERY_HEADS * HEAD_SIZE
    key_feature_width = KEY_VALUE_HEADS * HEAD_SIZE
    score_scale = 1.0 / math.sqrt(HEAD_SIZE)
    down_portion = adapter_down_weight.shape[2]
    up_portion = adapter_up_weight.shape[2]
    owned_token_slices = jnp.concatenate([adapter_down_weight, adapter_up_weight], axis=2)
    every_slice = lax.all_gather(owned_token_slices, "seq", axis=0, tiled=True)
    selected_tenant = lax.dynamic_index_in_dim(
        sequence_adapter_list, group_index, 0, keepdims=False
    )
    picked = jnp.take(every_slice, selected_tenant, axis=0)
    spread = lax.all_gather(picked[None], "ctx", axis=0, tiled=True)
    down_full = jnp.transpose(spread[:, :, :, :down_portion], (1, 2, 0, 3)).reshape(
        PICK, ADAPTER_RANK, MODEL_WIDTH
    )
    up_full = jnp.transpose(spread[:, :, :, down_portion:], (1, 2, 0, 3)).reshape(
        PICK, ADAPTER_RANK, query_width
    )
    block_count = row_total_count // TB
    slot_ids = tenant_block_entry[0]
    down_blocks = jnp.take(down_full, slot_ids, axis=0)
    up_blocks = jnp.take(up_full, slot_ids, axis=0)
    token_blocks = tokens.reshape(block_count, TB, MODEL_WIDTH)
    low_rank = jnp.einsum(
        "btd,brd->btr", token_blocks, down_blocks, preferred_element_type=jnp.float32
    ).astype(jnp.bfloat16)
    lifted = jnp.einsum("btr,brq->btq", low_rank, up_blocks, preferred_element_type=jnp.float32)
    query_rows = (
        frozen_query_base[0].astype(jnp.float32) + lifted.reshape(row_total_count, query_width)
    ).astype(jnp.bfloat16)
    query_head_rows = query_rows.reshape(
        row_total_count, KEY_VALUE_HEADS, head_groupings, HEAD_SIZE
    )
    query_pos = cycle_index * row_total_count + jnp.arange(row_total_count, dtype=jnp.int32)
    query_doc = document_numbers[0]
    start_forward = (
        jnp.full(
            (KEY_VALUE_HEADS, head_groupings, row_total_count), masked_fill_value, jnp.float32
        ),
        jnp.zeros((KEY_VALUE_HEADS, head_groupings, row_total_count), jnp.float32),
        jnp.zeros((KEY_VALUE_HEADS, head_groupings, row_total_count, HEAD_SIZE), jnp.float32),
    )
    gathered = (
        lax.all_gather(key_head_states[0], "ctx", axis=0, tiled=True),
        lax.all_gather(value_head_states[0], "ctx", axis=0, tiled=True),
        lax.all_gather(document_numbers[0], "ctx", axis=0, tiled=True),
    )
    key_piece, value_piece, doc_piece = gathered
    length = key_piece.shape[0]
    tenant_block_width = math.gcd(length, 512)

    def forward_one_block(block_index, state_now):
        first_row = block_index * tenant_block_width
        key_block = lax.dynamic_slice_in_dim(key_piece, first_row, tenant_block_width, 0).reshape(
            tenant_block_width, KEY_VALUE_HEADS, HEAD_SIZE
        )
        value_block = lax.dynamic_slice_in_dim(
            value_piece, first_row, tenant_block_width, 0
        ).reshape(tenant_block_width, KEY_VALUE_HEADS, HEAD_SIZE)
        doc_block = lax.dynamic_slice_in_dim(doc_piece, first_row, tenant_block_width, 0)
        key_pos = 0 + first_row + jnp.arange(tenant_block_width, dtype=jnp.int32)
        return forward_block(
            state_now,
            query_head_rows,
            query_pos,
            query_doc,
            key_block,
            value_block,
            doc_block,
            key_pos,
            score_scale,
        )

    running = lax.fori_loop(0, length // tenant_block_width, forward_one_block, start_forward)
    row_peak, weight_total, mixed_sum = running
    attention_row_block = (
        (mixed_sum / weight_total[..., None])
        .transpose(2, 0, 1, 3)
        .reshape(row_total_count, query_width)
        .astype(jnp.bfloat16)
    )
    log_total = row_peak + jnp.log(weight_total)
    gradient_row_block = output_gradient[0]
    gradient_head_rows = gradient_row_block.reshape(
        row_total_count, KEY_VALUE_HEADS, head_groupings, HEAD_SIZE
    )
    output_head_rows = attention_row_block.reshape(
        row_total_count, KEY_VALUE_HEADS, head_groupings, HEAD_SIZE
    )
    delta_sum = jnp.einsum(
        "tkgd,tkgd->kgt", gradient_head_rows, output_head_rows, preferred_element_type=jnp.float32
    )
    start_backward = (
        jnp.zeros((KEY_VALUE_HEADS, head_groupings, row_total_count, HEAD_SIZE), jnp.float32),
        jnp.zeros((seq_len, key_feature_width), jnp.float32),
        jnp.zeros((seq_len, key_feature_width), jnp.float32),
    )
    backward_key_piece, backward_value_piece, backward_doc_piece = gathered
    length = backward_key_piece.shape[0]
    backward_tenant_block_width = math.gcd(length, 512)

    def backward_one_block(block_index, state_now):
        query_sum, key_gradient_sum, value_gradient_sum = state_now
        first_row = block_index * backward_tenant_block_width
        key_block = lax.dynamic_slice_in_dim(
            backward_key_piece, first_row, backward_tenant_block_width, 0
        ).reshape(backward_tenant_block_width, KEY_VALUE_HEADS, HEAD_SIZE)
        value_block = lax.dynamic_slice_in_dim(
            backward_value_piece, first_row, backward_tenant_block_width, 0
        ).reshape(backward_tenant_block_width, KEY_VALUE_HEADS, HEAD_SIZE)
        doc_block = lax.dynamic_slice_in_dim(
            backward_doc_piece, first_row, backward_tenant_block_width, 0
        )
        row_start = 0 + first_row
        key_pos = row_start + jnp.arange(backward_tenant_block_width, dtype=jnp.int32)
        query_part, key_part, value_part = backward_block(
            query_head_rows,
            gradient_head_rows,
            query_pos,
            query_doc,
            log_total,
            delta_sum,
            key_block,
            value_block,
            doc_block,
            key_pos,
            score_scale,
        )
        old_key = lax.dynamic_slice_in_dim(
            key_gradient_sum, row_start, backward_tenant_block_width, 0
        )
        key_gradient_sum = lax.dynamic_update_slice_in_dim(
            key_gradient_sum,
            old_key + key_part.reshape(backward_tenant_block_width, key_feature_width),
            row_start,
            0,
        )
        old_value = lax.dynamic_slice_in_dim(
            value_gradient_sum, row_start, backward_tenant_block_width, 0
        )
        value_gradient_sum = lax.dynamic_update_slice_in_dim(
            value_gradient_sum,
            old_value + value_part.reshape(backward_tenant_block_width, key_feature_width),
            row_start,
            0,
        )
        return (query_sum + query_part, key_gradient_sum, value_gradient_sum)

    backward_sums = lax.fori_loop(
        0, length // backward_tenant_block_width, backward_one_block, start_backward
    )
    query_sum, key_rows_grad, value_rows_grad = backward_sums
    query_grad_low = (
        query_sum.transpose(2, 0, 1, 3).reshape(row_total_count, query_width).astype(jnp.bfloat16)
    )
    grad_blocks = query_grad_low.reshape(block_count, TB, query_width)
    low_grad = jnp.einsum(
        "btq,brq->btr", grad_blocks, up_blocks, preferred_element_type=jnp.float32
    ).astype(jnp.bfloat16)
    up_grad_blocks = jnp.einsum(
        "btr,btq->brq", low_rank, grad_blocks, preferred_element_type=jnp.float32
    )
    down_grad_blocks = jnp.einsum(
        "btr,btd->brd", low_grad, token_blocks, preferred_element_type=jnp.float32
    )
    down_sum = (
        jnp.zeros((PICK, ADAPTER_RANK, MODEL_WIDTH), jnp.float32).at[slot_ids].add(down_grad_blocks)
    )
    up_sum = (
        jnp.zeros((PICK, ADAPTER_RANK, query_width), jnp.float32).at[slot_ids].add(up_grad_blocks)
    )
    adapter_terms = jnp.concatenate(
        [
            down_sum.reshape(PICK, ADAPTER_RANK, cycle_count, down_portion).transpose(2, 0, 1, 3),
            up_sum.reshape(PICK, ADAPTER_RANK, cycle_count, up_portion).transpose(2, 0, 1, 3),
        ],
        axis=3,
    )
    key_share, value_share, adapter_part = (
        lax.psum_scatter(key_rows_grad, "ctx", scatter_dimension=0, tiled=True),
        lax.psum_scatter(value_rows_grad, "ctx", scatter_dimension=0, tiled=True),
        lax.psum_scatter(adapter_terms, "ctx", scatter_dimension=0, tiled=True),
    )
    adapter_share = adapter_part[0]
    owner_table = (
        jnp.zeros((every_slice.shape[0], ADAPTER_RANK, adapter_share.shape[2]), jnp.float32)
        .at[selected_tenant]
        .set(adapter_share)
    )
    owner_share = lax.psum_scatter(owner_table, "seq", scatter_dimension=0, tiled=True)
    down_grad = owner_share[:, :, :down_portion]
    up_grad = owner_share[:, :, down_portion:]
    return (attention_row_block[None], key_share[None], value_share[None], down_grad, up_grad)


def solution(mesh):
    in_specs = (
        P("seq", "ctx", None),
        P("seq", "ctx", None),
        P("seq", "ctx", None),
        P("seq", "ctx", None),
        P("seq", "ctx"),
        P("seq", "ctx"),
        P(),
        P("seq", None, "ctx"),
        P("seq", None, "ctx"),
        P("seq", "ctx", None),
    )
    out_specs = (
        P("seq", "ctx", None),
        P("seq", "ctx", None),
        P("seq", "ctx", None),
        P("seq", None, "ctx"),
        P("seq", None, "ctx"),
    )
    return jax.shard_map(
        per_device, mesh=mesh, in_specs=in_specs, out_specs=out_specs, check_vma=False
    )
```

profile of v0, /device:TPU:8, one launch (start us, length us, event | category | flops | bytes accessed | tf_op | source)
XLA Modules:
  0.0 1046.2 jit_solution(15468660724500184358)
XLA Ops:
  9.0 24.9 %all_gather.17 = bf16[16,64,384]{2,1,0:T(8,128)(2,1)S(1)} all-gather(bf16[1,64,384]{2,1,0:T(8,128)(2,1)S(1)} %pad_maximum_fusion.1), channel_id=1, replica_groups=mesh['ctx'=16,'seq'=16] {'seq'}, dimensions={0}, use_global_device_ids=true | all-gather | bytes 835584 | tf_op jit(solution)/shard_map/all_gather | solution.py:113
  42.2 35.4 %all-gather = s32[1,2048]{1,0:T(1,128)S(1)} all-gather(s32[1,128]{1,0:T(1,128)S(1)} %copy-done.16), channel_id=2, replica_groups=mesh['ctx'=16,'seq'=16] {'ctx'}, dimensions={1}, use_global_device_ids=true | all-gather | bytes 8704 | tf_op jit(solution)/shard_map/all_gather | solution.py:152
  77.6 68.5 %all-gather.7.cloned.1.call-done = bf16[16,6,64,384]{3,2,1,0:T(8,128)(2,1)} async-done(((bf16[1,6,64,384]{3,2,1,0:T(8,128)(2,1)}), bf16[16,6,64,384]{3,2,1,0:T(8,128)(2,1)}) %all-gather.7.cloned.1.call-update) | async-done | bytes 4718608 | tf_op jit(solution)/shard_map/all_gather | solution.py:118
  150.5 3.9 gather_fusion.1
  154.4 2.8 copy_bitcast_fusion
  159.3 2.7 fusion.34
  169.1 61.5 %all-gather.9.cloned.1.call-done = bf16[1,2048,512]{1,2,0:T(8,128)(2,1)} async-done(((bf16[1,128,512]{1,2,0:T(8,128)(2,1)}), bf16[1,2048,512]{1,2,0:T(8,128)(2,1)}) %all-gather.9.cloned.1.call-update) | async-done | bytes 2097168 | tf_op jit(solution)/shard_map/all_gather | solution.py:150
  230.6 85.8 %all-gather.11.cloned.1.call-done = bf16[1,2048,512]{1,2,0:T(8,128)(2,1)} async-done(((bf16[1,128,512]{1,2,0:T(8,128)(2,1)}), bf16[1,2048,512]{1,2,0:T(8,128)(2,1)}) %all-gather.11.cloned.1.call-update) | async-done | bytes 2097168 | tf_op jit(solution)/shard_map/all_gather | solution.py:151
  316.3 42.3 %while.36 = (s32[]{:T(128)}, f32[4,4,128]{2,1,0:T(4,128)S(1)}, f32[4,4,128]{2,1,0:T(4,128)S(1)}, f32[4,4,128,128]{3,2,1,0:T(8,128)}, s32[1,128]{1,0:T(1,128)S(1)...) while((s32[]{:T(128)}, f32[4,4,128]{2,1,0:T(4,128)S(1)}, ...), condition=%wide.region_3.4_spmd.clone, body=%wide.region_0.0_spmd.clone.sunk | while | flops 551496320 | bytes 43921192 | solution.py:180
  317.9 2.8 fusion.95
  320.7 3.3 fusion.96
  328.5 2.8 fusion.95
  331.3 3.3 fusion.96
  339.1 2.8 fusion.95
  341.9 3.3 fusion.96
  349.7 2.8 fusion.95
  352.5 3.3 fusion.96
  362.6 2.6 broadcast.152.clone
  367.7 132.2 %while.37 = (s32[]{:T(128)}, f32[4,4,128,128]{3,2,1,0:T(8,128)}, f32[2048,512]{1,0:T(8,128)}, f32[2048,512]{1,0:T(8,128)}, s32[1,128]{1,0:T(1,128)S(1)}, /*index...) while((s32[]{:T(128)}, f32[4,4,128,128]{3,2,1,0:T(8,128)}, ...), condition=%wide.region_5.6_spmd.clone, body=%wide.region_4.5_spmd.clone.sunk | while | flops 1356530304 | bytes 85692320 | solution.py:255
  374.3 2.9 fusion.111
  379.5 2.5 copy.120
  382.0 3.6 fusion.112
  386.8 2.6 copy.121
  391.6 2.5 copy.122
  407.0 3.3 fusion.111
  412.5 2.5 copy.120
  415.1 3.6 fusion.112
  419.9 2.6 copy.121
  424.7 2.5 copy.122
  440.1 3.3 fusion.111
  448.2 3.6 fusion.112
  453.0 2.6 copy.121
  457.8 2.5 copy.122
  473.3 3.3 fusion.111
  481.4 3.6 fusion.112
  486.2 2.6 copy.121
  491.0 2.5 copy.122
  503.9 3.1 fusion.37
  509.2 4.0 scatter_fusion.1
  517.8 3.4 broadcast_in_dim.144
  521.2 9.0 scatter_fusion
  530.2 5.6 copy.113
  536.5 2.9 pad_maximum_fusion
  539.4 6.5 copy.74
  546.1 206.1 %reduce-scatter.9.cloned.1.call-done = f32[1,6,64,384]{3,2,1,0:T(8,128)} async-done(((f32[16,6,64,384]{3,2,1,0:T(8,128)}), f32[1,6,64,384]{3,2,1,0:T(8,128)}) %reduce-scatter.9.cloned.1.call-update) | async-done | bytes 589840 | tf_op jit(solution)/shard_map/reduce_scatter | solution.py:288
  758.2 75.2 %reduce-scatter.11.cloned.1.call-done = f32[1,64,384]{2,1,0:T(8,128)} async-done(((f32[16,64,384]{2,1,0:T(8,128)}), f32[1,64,384]{2,1,0:T(8,128)}) %reduce-scatter.11.cloned.1.call-update) | async-done | bytes 98320 | tf_op jit(solution)/shard_map/reduce_scatter | solution.py:296
  836.2 99.8 %reduce-scatter.5.cloned.1.call-done = f32[128,512]{1,0:T(8,128)} async-done(((f32[2048,512]{1,0:T(8,128)}), f32[128,512]{1,0:T(8,128)}) %reduce-scatter.5.cloned.1.call-update) | async-done | bytes 262160 | tf_op jit(solution)/shard_map/reduce_scatter | solution.py:286
  936.1 103.3 %reduce-scatter.7.cloned.1.call-done = f32[128,512]{1,0:T(8,128)} async-done(((f32[2048,512]{1,0:T(8,128)}), f32[128,512]{1,0:T(8,128)}) %reduce-scatter.7.cloned.1.call-update) | async-done | bytes 262160 | tf_op jit(solution)/shard_map/reduce_scatter | solution.py:287
  (251 shorter events, 146.9 us)
Async XLA Ops:
  7.2 152.1 %copy-start = (bf16[1,128,4096]{2,1,0:T(8,128)(2,1)S(1)}, bf16[1,128,4096]{2,1,0:T(8,128)(2,1)}, u32[]{:S(2)}) copy-start(bf16[1,128,4096]{2,1,0:T(8,128)(2,1)} %param.14) | copy-start | bytes 3145732
  7.2 34.0 %copy-start.15 = (bf16[1,128,2048]{2,1,0:T(8,128)(2,1)S(1)}, bf16[1,128,2048]{2,1,0:T(8,128)(2,1)}, u32[]{:S(2)}) copy-start(bf16[1,128,2048]{2,1,0:T(8,128)(2,1)} %param.23) | copy-start | bytes 1572868
  7.2 35.0 %copy-start.16 = (s32[1,128]{1,0:T(1,128)S(1)}, s32[1,128]{1,0:T(1,128)}, u32[]{:S(2)}) copy-start(s32[1,128]{1,0:T(1,128)} %param.18) | copy-start | bytes 1540
  7.2 70.4 %copy-start.19 = (s32[1,4]{1,0:T(1,128)S(1)}, s32[1,4]{1,0:T(1,128)}, u32[]{:S(2)}) copy-start(s32[1,4]{1,0:T(1,128)} %param.19) | copy-start | bytes 52
  7.2 138.9 %all-gather.7.cloned.1.call-start = ((), (), s32[]{:S(2)}) async-start(), calls=%async_computation.4 | async-start | bytes 5013504 | tf_op jit(solution)/shard_map/all_gather | solution.py:118
  8.2 25.7 %copy-start.17 = (s32[6]{0:T(128)}, s32[6]{0:T(128)S(1)}, u32[]{:S(2)}) copy-start(s32[6]{0:T(128)S(1)} %fusion.40) | copy-start | bytes 76
  35.4 195.2 %all-gather.9.cloned.1.call-start = ((), (), s32[]{:S(2)}) async-start(), calls=%async_computation.9 | async-start | bytes 2228224 | tf_op jit(solution)/shard_map/all_gather | solution.py:150
  37.1 279.2 %all-gather.11.cloned.1.call-start = ((), (), s32[]{:S(2)}) async-start(), calls=%async_computation.10 | async-start | bytes 2228224 | tf_op jit(solution)/shard_map/all_gather | solution.py:151
  38.9 713.3 %reduce-scatter.9.cloned.1.call-start = ((), (), s32[]{:S(2)}) async-start(), calls=%async_computation.7 | async-start | bytes 10027008 | tf_op jit(solution)/shard_map/reduce_scatter | solution.py:288
  159.2 4.8 copy-start.7
  317.9 6.2 copy-start.13
  320.7 3.4 copy-start.1
  328.5 6.2 copy-start.13
  331.3 3.4 copy-start.1
  339.1 6.2 copy-start.13
  341.9 3.4 copy-start.1
  349.6 6.2 copy-start.13
  352.5 3.4 copy-start.1
  367.7 5.0 copy-start.11
  368.8 3.6 copy-start.2
  370.8 3.5 copy-start.3
  382.0 3.6 copy-start.5
  394.2 1.9 copy-start.6
  396.1 2.8 copy-start.4
  400.4 5.0 copy-start.11
  401.5 3.6 copy-start.2
  403.5 3.4 copy-start.3
  415.1 3.6 copy-start.5
  427.2 1.9 copy-start.6
  429.2 2.8 copy-start.4
  433.5 5.0 copy-start.11
  434.6 3.6 copy-start.2
  436.6 3.5 copy-start.3
  448.2 3.6 copy-start.5
  460.4 1.9 copy-start.6
  462.3 2.8 copy-start.4
  466.7 5.0 copy-start.11
  467.8 3.6 copy-start.2
  469.8 3.4 copy-start.3
  481.4 3.6 copy-start.5
  493.6 1.9 copy-start.6
  495.5 2.8 copy-start.4
  499.9 4.1 copy-start.8
  507.0 2.2 copy-start.10
  546.0 206.3 %copy-start.18 = (s32[6]{0:T(128)S(1)}, s32[6]{0:T(128)}, u32[]{:S(2)}) copy-start(s32[6]{0:T(128)} %copy-done.17) | copy-start | bytes 76
  546.0 287.4 %reduce-scatter.11.cloned.1.call-start = ((), (), s32[]{:S(2)}) async-start(), calls=%async_computation.8 | async-start | bytes 1671168 | tf_op jit(solution)/shard_map/reduce_scatter | solution.py:296
  755.3 180.8 %reduce-scatter.5.cloned.1.call-start = ((), (), s32[]{:S(2)}) async-start(), calls=%async_computation.5 | async-start | bytes 4456448 | tf_op jit(solution)/shard_map/reduce_scatter | solution.py:286
  755.9 283.5 %reduce-scatter.7.cloned.1.call-start = ((), (), s32[]{:S(2)}) async-start(), calls=%async_computation.6 | async-start | bytes 4456448 | tf_op jit(solution)/shard_map/reduce_scatter | solution.py:287
  (6 other events, 6.6 us)
Sparse Core Ops, SparseCore 0:
  35.5 110.5 all-gather.6
  148.4 82.0 all-gather.8
  232.9 83.4 all-gather.10
  546.1 205.9 reduce-scatter.8
  756.2 77.1 reduce-scatter.10
  836.5 99.4 reduce-scatter.4
  939.4 99.9 reduce-scatter.6
where the time goes:
time: 1050 us
  waiting for transfers between devices  701 us (67%)
  local copies, waits for them, and re-layouts  145 us (14%)
  matrix products  75.2 us (7%)
  blocking collectives  60.3 us (6%)
  other arithmetic  49.3 us (5%)
  between operations  14.4 us (1%)
    reduce_scatter x1, waiting for transfers between devices, per_device(): lax.psum_scatter(adapter_terms, 'ctx', scatter_dimension=0, tiled=True)  206 us
    reduce_scatter x1, waiting for transfers between devices, per_device(): lax.psum_scatter(value_rows_grad, 'ctx', scatter_dimension=0, tiled=True)  103 us
    reduce_scatter x1, waiting for transfers between devices, per_device(): lax.psum_scatter(key_rows_grad, 'ctx', scatter_dimension=0, tiled=True)  99.8 us
    all_gather x1, waiting for transfers between devices, per_device(): lax.all_gather(value_head_states[0], 'ctx', axis=0, tiled=True)  85.8 us
    reduce_scatter x1, waiting for transfers between devices, per_device(): lax.psum_scatter(owner_table, 'seq', scatter_dimension=0, tiled=True)  75.2 us
    all_gather x1, waiting for transfers between devices, per_device(): spread = lax.all_gather(picked[None], 'ctx', axis=0, tiled=True)  68.5 us
    all_gather x1, waiting for transfers between devices, per_device(): lax.all_gather(key_head_states[0], 'ctx', axis=0, tiled=True)  61.5 us
    all_gather x1, blocking collectives, per_device(): lax.all_gather(document_numbers[0], 'ctx', axis=0, tiled=True)  35.4 us
  transfers between devices with their start and end apart: 7, of which 7 were waited for; matrix products, arithmetic and copies ran while one was open for 3% of the time, Pallas kernels for 0%

commit v1 on v0

--- a/solution.py
+++ b/solution.py
@@ -97,6 +97,13 @@
     adapter_up_weight,
     output_gradient,
 ):
+
+    def rest_stages_all(local_x, mesh_name, d0):
+        step_out = lax.psum(1, mesh_name)
+        return jnp.concatenate(
+            lax.all_to_all(jnp.stack(step_out * [local_x], axis=0), mesh_name, 0, 0), axis=d0
+        )
+
     cycle_count = lax.axis_size("ctx")
     cycle_index = lax.axis_index("ctx")
     group_index = lax.axis_index("seq")
@@ -148,7 +155,7 @@
     )
     gathered = (
         lax.all_gather(key_head_states[0], "ctx", axis=0, tiled=True),
-        lax.all_gather(value_head_states[0], "ctx", axis=0, tiled=True),
+        rest_stages_all(value_head_states[0], "ctx", 0),
         lax.all_gather(document_numbers[0], "ctx", axis=0, tiled=True),
     )
     key_piece, value_piece, doc_piece = gathered

time: 1050 us -> 992 us (0.945)
  waiting for transfers between devices: 701 us -> 577 us
  blocking collectives: 60.3 us -> 112 us
    all_gather x1 -> x0, waiting for transfers between devices: 85.8 us -> none  [per_device(): lax.all_gather(value_head_states[0], 'ctx', axis=0, tiled=True)]
    all_gather x1, blocking collectives: 35.4 us -> 87.1 us  [per_device(): lax.all_gather(document_numbers[0], 'ctx', axis=0, tiled=True)]
    all_gather x1, waiting for transfers between devices: 68.5 us -> 34.1 us  [per_device(): spread = lax.all_gather(picked[None], 'ctx', axis=0, tiled=True)]
  transfers between devices with their start and end apart: 7 -> 7, of which waited for: 7 -> 6; matrix products, arithmetic and copies ran while one was open for 3% -> 4% of each run, Pallas kernels for 0% -> 0%
where the time goes in v1:
time: 992 us; the launch traced here: 990 us
  waiting for transfers between devices  577 us (58%)
  local copies, waits for them, and re-layouts  152 us (15%)
  blocking collectives  112 us (11%)
  matrix products  75.1 us (8%)
  other arithmetic  49.3 us (5%)
  between operations  14.4 us (1%)
    reduce_scatter x1, waiting for transfers between devices, per_device(): lax.psum_scatter(adapter_terms, 'ctx', scatter_dimension=0, tiled=True)  205 us
    reduce_scatter x1, waiting for transfers between devices, per_device(): lax.psum_scatter(value_rows_grad, 'ctx', scatter_dimension=0, tiled=True)  103 us
    reduce_scatter x1, waiting for transfers between devices, per_device(): lax.psum_scatter(key_rows_grad, 'ctx', scatter_dimension=0, tiled=True)  99.9 us
    all_gather x1, blocking collectives, per_device(): lax.all_gather(document_numbers[0], 'ctx', axis=0, tiled=True)  87.1 us
    reduce_scatter x1, waiting for transfers between devices, per_device(): lax.psum_scatter(owner_table, 'seq', scatter_dimension=0, tiled=True)  75.4 us
    all_gather x1, waiting for transfers between devices, per_device(): lax.all_gather(key_head_states[0], 'ctx', axis=0, tiled=True)  58.8 us
    all_gather x1, waiting for transfers between devices, per_device(): spread = lax.all_gather(picked[None], 'ctx', axis=0, tiled=True)  34.1 us
    all_gather x1, blocking collectives, per_device(): every_slice = lax.all_gather(owned_token_slices, 'seq', axis=0, tiled=True)  24.9 us
  transfers between devices with their start and end apart: 7, of which 6 were waited for; matrix products, arithmetic and copies ran while one was open for 4% of the time, Pallas kernels for 0%

profile of v1, /device:TPU:8, one launch (start us, length us, event | category | flops | bytes accessed | tf_op | source)
XLA Modules:
  0.0 989.5 jit_solution(2069719634484015387)
XLA Ops:
  9.0 24.9 %all_gather.14 = bf16[16,64,384]{2,1,0:T(8,128)(2,1)S(1)} all-gather(bf16[1,64,384]{2,1,0:T(8,128)(2,1)S(1)} %pad_maximum_fusion.1), channel_id=1, replica_groups=mesh['ctx'=16,'seq'=16] {'seq'}, dimensions={0}, use_global_device_ids=true | all-gather | bytes 835584 | tf_op jit(solution)/shard_map/all_gather | solution.py:120
  38.2 8.6 all-to-all-start
  51.9 87.1 %all-gather = s32[1,2048]{1,0:T(1,128)S(1)} all-gather(s32[1,128]{1,0:T(1,128)S(1)} %copy-done.16), channel_id=2, replica_groups=mesh['ctx'=16,'seq'=16] {'ctx'}, dimensions={1}, use_global_device_ids=true | all-gather | bytes 8704 | tf_op jit(solution)/shard_map/all_gather | solution.py:159
  139.0 2.6 copy.92
  141.7 3.9 copy.94
  145.6 34.1 %all-gather.5.cloned.1.call-done = bf16[16,6,64,384]{3,2,1,0:T(8,128)(2,1)} async-done(((bf16[1,6,64,384]{3,2,1,0:T(8,128)(2,1)}), bf16[16,6,64,384]{3,2,1,0:T(8,128)(2,1)}) %all-gather.5.cloned.1.call-update) | async-done | bytes 4718608 | tf_op jit(solution)/shard_map/all_gather | solution.py:125
  184.1 3.9 gather_fusion.1
  187.9 2.8 copy_bitcast_fusion
  192.8 2.7 fusion.34
  202.7 58.8 %all-gather.7.cloned.1.call-done = bf16[1,2048,512]{1,2,0:T(8,128)(2,1)} async-done(((bf16[1,128,512]{1,2,0:T(8,128)(2,1)}), bf16[1,2048,512]{1,2,0:T(8,128)(2,1)}) %all-gather.7.cloned.1.call-update) | async-done | bytes 2097168 | tf_op jit(solution)/shard_map/all_gather | solution.py:157
  261.5 42.2 %while.36 = (s32[]{:T(128)}, f32[4,4,128]{2,1,0:T(4,128)S(1)}, f32[4,4,128]{2,1,0:T(4,128)S(1)}, f32[4,4,128,128]{3,2,1,0:T(8,128)}, s32[1,128]{1,0:T(1,128)S(1)...) while((s32[]{:T(128)}, f32[4,4,128]{2,1,0:T(4,128)S(1)}, ...), condition=%wide.region_3.4_spmd.clone, body=%wide.region_0.0_spmd.clone.sunk | while | flops 551496320 | bytes 43921192 | solution.py:187
  263.1 2.8 fusion.95
  265.9 3.3 fusion.96
  273.6 2.8 fusion.95
  276.5 3.3 fusion.96
  284.2 2.8 fusion.95
  287.0 3.3 fusion.96
  294.7 2.8 fusion.95
  297.6 3.3 fusion.96
  307.6 2.6 broadcast.153.clone
  312.7 132.2 %while.37 = (s32[]{:T(128)}, f32[4,4,128,128]{3,2,1,0:T(8,128)}, f32[2048,512]{1,0:T(8,128)}, f32[2048,512]{1,0:T(8,128)}, s32[1,128]{1,0:T(1,128)S(1)}, /*index...) while((s32[]{:T(128)}, f32[4,4,128,128]{3,2,1,0:T(8,128)}, ...), condition=%wide.region_5.6_spmd.clone, body=%wide.region_4.5_spmd.clone.sunk | while | flops 1356530304 | bytes 85692320 | solution.py:262
  319.3 2.9 fusion.111
  327.1 3.6 fusion.112
  331.9 2.6 copy.148
  336.7 2.6 copy.149
  352.1 3.3 fusion.111
  360.2 3.6 fusion.112
  364.9 2.6 copy.148
  369.8 2.6 copy.149
  385.2 3.3 fusion.111
  393.3 3.6 fusion.112
  398.1 2.6 copy.148
  402.9 2.6 copy.149
  418.4 3.3 fusion.111
  426.5 3.6 fusion.112
  431.3 2.6 copy.148
  436.1 2.6 copy.149
  449.0 3.1 fusion.37
  454.3 3.9 scatter_fusion.1
  462.9 3.4 broadcast_in_dim.144
  466.3 9.0 scatter_fusion
  475.3 5.6 copy.140
  481.6 2.9 pad_maximum_fusion
  484.5 6.5 copy.101
  491.2 204.8 %reduce-scatter.9.cloned.1.call-done = f32[1,6,64,384]{3,2,1,0:T(8,128)} async-done(((f32[16,6,64,384]{3,2,1,0:T(8,128)}), f32[1,6,64,384]{3,2,1,0:T(8,128)}) %reduce-scatter.9.cloned.1.call-update) | async-done | bytes 589840 | tf_op jit(solution)/shard_map/reduce_scatter | solution.py:295
  701.9 75.4 %reduce-scatter.11.cloned.1.call-done = f32[1,64,384]{2,1,0:T(8,128)} async-done(((f32[16,64,384]{2,1,0:T(8,128)}), f32[1,64,384]{2,1,0:T(8,128)}) %reduce-scatter.11.cloned.1.call-update) | async-done | bytes 98320 | tf_op jit(solution)/shard_map/reduce_scatter | solution.py:303
  780.1 99.9 %reduce-scatter.5.cloned.1.call-done = f32[128,512]{1,0:T(8,128)} async-done(((f32[2048,512]{1,0:T(8,128)}), f32[128,512]{1,0:T(8,128)}) %reduce-scatter.5.cloned.1.call-update) | async-done | bytes 262160 | tf_op jit(solution)/shard_map/reduce_scatter | solution.py:293
  879.9 102.7 %reduce-scatter.7.cloned.1.call-done = f32[128,512]{1,0:T(8,128)} async-done(((f32[2048,512]{1,0:T(8,128)}), f32[128,512]{1,0:T(8,128)}) %reduce-scatter.7.cloned.1.call-update) | async-done | bytes 262160 | tf_op jit(solution)/shard_map/reduce_scatter | solution.py:294
  (253 shorter events, 153.1 us)
Async XLA Ops:
  7.2 185.7 %copy-start = (bf16[1,128,4096]{2,1,0:T(8,128)(2,1)S(1)}, bf16[1,128,4096]{2,1,0:T(8,128)(2,1)}, u32[]{:S(2)}) copy-start(bf16[1,128,4096]{2,1,0:T(8,128)(2,1)} %param.14) | copy-start | bytes 3145732
  7.2 172.5 %all-gather.5.cloned.1.call-start = ((), (), s32[]{:S(2)}) async-start(), calls=%async_computation.5 | async-start | bytes 5013504 | tf_op jit(solution)/shard_map/all_gather | solution.py:125
  8.2 25.7 %copy-start.17 = (s32[6]{0:T(128)}, s32[6]{0:T(128)S(1)}, u32[]{:S(2)}) copy-start(s32[6]{0:T(128)S(1)} %fusion.40) | copy-start | bytes 76
  33.9 12.9 %copy-start.15 = (bf16[1,128,512]{2,1,0:T(8,128)(2,1)S(1)}, bf16[1,128,512]{2,1,0:T(8,128)(2,1)}, u32[]{:S(2)}) copy-start(bf16[1,128,512]{2,1,0:T(8,128)(2,1)} %param.16) | copy-start | bytes 393220
  36.4 15.6 %copy-start.16 = (s32[1,128]{1,0:T(1,128)S(1)}, s32[1,128]{1,0:T(1,128)}, u32[]{:S(2)}) copy-start(s32[1,128]{1,0:T(1,128)} %param.18) | copy-start | bytes 1540
  36.4 102.6 %copy-start.19 = (s32[1,4]{1,0:T(1,128)S(1)}, s32[1,4]{1,0:T(1,128)}, u32[]{:S(2)}) copy-start(s32[1,4]{1,0:T(1,128)} %param.19) | copy-start | bytes 52
  38.2 100.9 %all-to-all-start = ((bf16[16,128,512]{1,2,0:T(8,128)(2,1)}), bf16[16,128,512]{1,2,0:T(8,128)(2,1)S(1)}, u32[]{:S(2)}, u32[]{:S(2)}) async-start(bf16[16,128,512]{1,2,0:T(8,128)(2,1)} %stack.3), calls=%async_computation | async-start | bytes 4194304 | tf_op jit(solution)/shard_map/all_to_all | solution.py:104
  46.7 214.8 %all-gather.7.cloned.1.call-start = ((), (), s32[]{:S(2)}) async-start(), calls=%async_computation.10 | async-start | bytes 2228224 | tf_op jit(solution)/shard_map/all_gather | solution.py:157
  47.6 648.4 %reduce-scatter.9.cloned.1.call-start = ((), (), s32[]{:S(2)}) async-start(), calls=%async_computation.8 | async-start | bytes 10027008 | tf_op jit(solution)/shard_map/reduce_scatter | solution.py:295
  192.8 4.8 copy-start.7
  263.1 6.2 copy-start.13
  265.9 3.4 copy-start.1
  273.6 6.2 copy-start.13
  276.4 3.4 copy-start.1
  284.2 6.2 copy-start.13
  287.0 3.4 copy-start.1
  294.7 6.2 copy-start.13
  297.6 3.4 copy-start.1
  312.7 5.0 copy-start.11
  313.9 3.6 copy-start.2
  315.9 3.4 copy-start.3
  327.1 3.6 copy-start.5
  339.2 1.9 copy-start.6
  341.2 2.8 copy-start.4
  345.5 5.0 copy-start.11
  346.6 3.6 copy-start.2
  348.6 3.4 copy-start.3
  360.2 3.6 copy-start.5
  372.3 2.0 copy-start.6
  374.3 2.8 copy-start.4
  378.6 5.0 copy-start.11
  379.7 3.6 copy-start.2
  381.7 3.5 copy-start.3
  393.3 3.6 copy-start.5
  405.4 1.9 copy-start.6
  407.4 2.8 copy-start.4
  411.8 5.0 copy-start.11
  412.9 3.6 copy-start.2
  414.9 3.4 copy-start.3
  426.5 3.6 copy-start.5
  438.7 2.0 copy-start.6
  440.6 2.8 copy-start.4
  445.0 4.1 copy-start.8
  452.2 2.2 copy-start.10
  491.1 205.0 %copy-start.18 = (s32[6]{0:T(128)S(1)}, s32[6]{0:T(128)}, u32[]{:S(2)}) copy-start(s32[6]{0:T(128)} %copy-done.17) | copy-start | bytes 76
  491.1 286.1 %reduce-scatter.11.cloned.1.call-start = ((), (), s32[]{:S(2)}) async-start(), calls=%async_computation.9 | async-start | bytes 1671168 | tf_op jit(solution)/shard_map/reduce_scatter | solution.py:303
  699.1 180.8 %reduce-scatter.5.cloned.1.call-start = ((), (), s32[]{:S(2)}) async-start(), calls=%async_computation.6 | async-start | bytes 4456448 | tf_op jit(solution)/shard_map/reduce_scatter | solution.py:293
  699.7 283.0 %reduce-scatter.7.cloned.1.call-start = ((), (), s32[]{:S(2)}) async-start(), calls=%async_computation.7 | async-start | bytes 4456448 | tf_op jit(solution)/shard_map/reduce_scatter | solution.py:294
  (6 other events, 6.4 us)
Sparse Core Ops, SparseCore 0:
  35.5 144.2 all-gather.4
  182.0 79.4 all-gather.6
  491.2 204.6 reduce-scatter.8
  700.0 77.1 reduce-scatter.10
  780.4 99.5 reduce-scatter.4
  883.1 99.5 reduce-scatter.6
